TPU v7x, 32 devices: a whole 2x2x4 slice. The times are simulated.
32 devices in a mesh: group: 2 (over y), frame: 4 (over z), space: 2 (over x), head: 2 (over core).
Axes of the slice: x: 2, y: 2, z: 4, core: 2. Of those that a mesh axis runs over, the one named last changes fastest.
Arguments:
- queries: bfloat16 [8, 8, 48, 3072], P(('group', 'frame'), 'space', None, 'head'), parts along dimension 0, may hold values from -8 to 8
- keys: bfloat16 [8, 8, 48, 3072], P(('group', 'frame'), 'space', None, 'head'), parts along dimension 0, may hold values from -8 to 8
- values: bfloat16 [8, 8, 48, 3072], P(('group', 'frame'), 'space', None, 'head'), parts along dimension 0, may hold values from -6 to 6
- flags: int32 [4, 4], replicated, may hold values from 0 to 1, as said below
- widths: int32 [4], replicated, may hold values from 0 to 8, as said below
Outputs:
- attended: bfloat16 [8, 8, 48, 3072], P(('group', 'frame'), 'space', None, 'head'), parts along dimension 0
There are 2 independent parts, one for each index of `group`. A program takes and returns all parts, laid end to end along the dimension named above; an argument that names none is the same for every part. Nothing has to cross between parts.
Inputs may be any that keep to these rules, and one draw needn't show every extreme that they name: flags[f, g] = 1 wherever |f - g| <= 1, and flags[0, 3] = flags[3, 0] = 0. widths[0] = 8, and widths never rise with the frame distance.
All inputs are finite; a program needn't handle non-finite values.
Results may differ from a plain program's by a relative error of at most 0.006.
Values may be sent and summed in bfloat16 or wider, within the bound.
A program may use at most 128 MiB of HBM per device.

v0:
```python
import jax
import jax.numpy as jnp
from jax import lax
from jax.sharding import PartitionSpec as P

HEAD_DIM = 128
NEG_FILL = -1e30


def empty_state(leading, head_count, query_count):
    return (
        jnp.full(leading + (head_count, query_count), NEG_FILL, jnp.float32),
        jnp.zeros(leading + (head_count, query_count), jnp.float32),
        jnp.zeros(leading + (head_count, query_count, HEAD_DIM), jnp.float32),
    )


def block_update(state_old, query_heads, query_rows, reach_rows, key_block, key_rows):
    running_max, running_total, running_acc = state_old
    query_count, head_count, head_size = query_heads.shape
    key_count = key_rows.shape[0]
    score_scale = 1.0 / HEAD_DIM**0.5
    allowed = jnp.abs(query_rows[:, None] - key_rows[None, :]) <= reach_rows
    key_heads = key_block[0].reshape(key_count, head_count, head_size)
    value_heads = key_block[1].reshape(key_count, head_count, head_size)
    scores = (
        jnp.einsum("qhd,khd->hqk", query_heads, key_heads, preferred_element_type=jnp.float32)
        * score_scale
    )
    scores = jnp.where(allowed[None], scores, NEG_FILL)
    new_max = jnp.maximum(running_max, jnp.max(scores, axis=2))
    weights = jnp.where(allowed[None], jnp.exp(scores - new_max[:, :, None]), 0.0)
    rescale = jnp.exp(running_max - new_max)
    new_total = running_total * rescale + jnp.sum(weights, axis=2)
    new_acc = running_acc * rescale[:, :, None] + jnp.einsum(
        "hqk,khd->hqd",
        weights.astype(jnp.bfloat16),
        value_heads,
        preferred_element_type=jnp.float32,
    )
    return (new_max, new_total, new_acc)


def shards(queries, keys, values, flags, widths):
    frame_now = lax.axis_index("frame")
    head_query, head_key, head_value = (
        lax.all_to_all(queries, "space", split_axis=3, concat_axis=1, tiled=True),
        lax.all_to_all(keys, "space", split_axis=3, concat_axis=1, tiled=True),
        lax.all_to_all(values, "space", split_axis=3, concat_axis=1, tiled=True),
    )
    row_total = head_query.shape[1]
    columns = head_query.shape[2]
    features = head_query.shape[3]
    head_count = features // HEAD_DIM
    frame_tokens = row_total * columns
    key_rows = jnp.arange(frame_tokens, dtype=jnp.int32) // columns
    stacked = jnp.stack(
        [head_key.reshape(frame_tokens, features), head_value.reshape(frame_tokens, features)],
        axis=0,
    )[None]
    query_heads = head_query.reshape(frame_tokens, head_count, HEAD_DIM)
    flag_row = lax.dynamic_index_in_dim(flags, frame_now, 0, False)
    initial = empty_state((), head_count, frame_tokens)
    key_piece = lax.all_gather(stacked, "frame", axis=0, tiled=True)

    def advance(state_old, step_items):
        key_block, offset_now = step_items
        reach_rows = lax.dynamic_index_in_dim(widths, jnp.abs(frame_now - offset_now), 0, False)
        flag_now = lax.dynamic_index_in_dim(flag_row, offset_now, 0, False)
        state_new = lax.cond(
            flag_now > 0,
            lambda kept_state: block_update(
                kept_state, query_heads, key_rows, reach_rows, key_block, key_rows
            ),
            lambda kept_state: kept_state,
            state_old,
        )
        return (state_new, None)

    state_new, unused = lax.scan(
        advance, initial, (key_piece, jnp.arange(key_piece.shape[0], dtype=jnp.int32))
    )
    final_max, final_total, final_acc = state_new
    blended = final_acc / final_total[:, :, None]
    joined = jnp.transpose(blended, (1, 0, 2)).reshape(head_query.shape).astype(jnp.bfloat16)
    return lax.all_to_all(joined, "space", split_axis=1, concat_axis=3, tiled=True)


def solution(mesh):
    placed = (
        P(("group", "frame"), "space", None, "head"),
        P(("group", "frame"), "space", None, "head"),
        P(("group", "frame"), "space", None, "head"),
        P(),
        P(),
    )
    return jax.shard_map(
        shards,
        mesh=mesh,
        in_specs=placed,
        out_specs=P(("group", "frame"), "space", None, "head"),
        check_vma=False,
    )
```

profile of v0, /device:TPU:16, one launch (start us, length us, event | category | flops | bytes accessed | tf_op | source)
XLA Modules:
  0.0 199.9 jit_solution(7581698430664993695)
XLA Ops:
  6.5 2.6 %copy.41 = bf16[1,4,48,1536]{2,1,0,3:T(4,128)(2,1)S(1)} copy(bf16[1,4,48,1536]{3,2,1,0:T(8,128)(2,1)} %param.11) | data formatting | bytes 1179648 | tf_op args[2]
  9.1 3.4 %reshape.68 = bf16[2,2,73728]{2,1,0:T(2,128)(2,1)} reshape(bf16[1536,1,4,48]{3,2,1,0:T(4,128)(2,1)S(1)} %bitcast.61) | data formatting | bytes 1179648
  12.5 3.5 %all-to-all-start.1 = ((bf16[2,2,73728]{2,1,0:T(2,128)(2,1)}), bf16[2,2,73728]{2,1,0:T(2,128)(2,1)S(1)}, u32[]{:S(2)}, u32[]{:S(2)}) async-start(bf16[2,2,73728]{2,1,0:T(2,128)(2,1)} %reshape.68), calls=%async_computation.1 | async-start | bytes 1179648 | tf_op jit(solution)/shard_map/all_to_all | solution.py:49
  16.0 1.0 copy.38
  17.1 3.4 %reshape.70 = bf16[2,2,73728]{2,1,0:T(2,128)(2,1)} reshape(bf16[1536,1,4,48]{3,2,1,0:T(4,128)(2,1)S(1)} %bitcast.62) | data formatting | bytes 1179648
  20.5 4.5 %all-to-all-done.1 = bf16[2,2,73728]{2,1,0:T(2,128)(2,1)S(1)} async-done(((bf16[2,2,73728]{2,1,0:T(2,128)(2,1)}), bf16[2,2,73728]{2,1,0:T(2,128)(2,1)S(1)}, u32[]{:S(2)}, u32[]{:S(2)}) %all-to-all-start.1) | async-done | bytes 589856 | tf_op jit(solution)/shard_map/all_to_all | solution.py:49
  25.0 3.5 %all-to-all-start = ((bf16[2,2,73728]{2,1,0:T(2,128)(2,1)}), bf16[2,2,73728]{2,1,0:T(2,128)(2,1)S(1)}, u32[]{:S(2)}, u32[]{:S(2)}) async-start(bf16[2,2,73728]{2,1,0:T(2,128)(2,1)} %reshape.70), calls=%async_computation | async-start | bytes 1179648 | tf_op jit(solution)/shard_map/all_to_all | solution.py:48
  28.5 1.6 reshape.69
  30.1 1.3 copy.55
  31.5 5.0 %all-to-all-done = bf16[2,2,73728]{2,1,0:T(2,128)(2,1)S(1)} async-done(((bf16[2,2,73728]{2,1,0:T(2,128)(2,1)}), bf16[2,2,73728]{2,1,0:T(2,128)(2,1)S(1)}, u32[]{:S(2)}, u32[]{:S(2)}) %all-to-all-start) | async-done | bytes 589856 | tf_op jit(solution)/shard_map/all_to_all | solution.py:48
  36.6 1.6 reshape.71
  38.1 1.3 copy.54
  39.6 1.1 pad_maximum_fusion
  40.7 1.0 copy.44
  41.8 3.4 %reshape.72 = bf16[2,2,73728]{2,1,0:T(2,128)(2,1)} reshape(bf16[1536,1,4,48]{3,2,1,0:T(4,128)(2,1)S(1)} %bitcast.63) | data formatting | bytes 1179648
  45.2 3.7 %all-to-all-start.2 = ((bf16[2,2,73728]{2,1,0:T(2,128)(2,1)}), bf16[2,2,73728]{2,1,0:T(2,128)(2,1)S(1)}, u32[]{:S(2)}, u32[]{:S(2)}) async-start(bf16[2,2,73728]{2,1,0:T(2,128)(2,1)} %reshape.72), calls=%async_computation.2 | async-start | bytes 1179648 | tf_op jit(solution)/shard_map/all_to_all | solution.py:47
  48.9 7.0 %all-to-all-done.2 = bf16[2,2,73728]{2,1,0:T(2,128)(2,1)S(1)} async-done(((bf16[2,2,73728]{2,1,0:T(2,128)(2,1)}), bf16[2,2,73728]{2,1,0:T(2,128)(2,1)S(1)}, u32[]{:S(2)}, u32[]{:S(2)}) %all-to-all-start.2) | async-done | bytes 589856 | tf_op jit(solution)/shard_map/all_to_all | solution.py:47
  55.9 1.6 reshape.73
  57.5 0.8 copy.45
  58.3 0.7 reshape.64
  59.0 69.8 %all-gather.3.cloned.1.call-done = bf16[8,384,768]{2,1,0:T(8,128)(2,1)} async-done(((bf16[2,384,768]{2,1,0:T(8,128)(2,1)}), bf16[8,384,768]{2,1,0:T(8,128)(2,1)}) %all-gather.3.cloned.1.call-update) | async-done | bytes 4718608 | tf_op jit(solution)/shard_map/all_gather | solution.py:64
  128.8 6.6 %copy.46 = bf16[4,2,384,768]{2,3,1,0:T(8,128)(2,1)} copy(bf16[4,2,384,768]{3,2,1,0:T(8,128)(2,1)} %bitcast.64) | data formatting | bytes 9437184
  135.6 43.9 %while.15 = (s32[]{:T(128)}, f32[6,384]{1,0:T(8,128)S(1)}, f32[6,384]{1,0:T(8,128)S(1)}, f32[6,384,128]{2,1,0:T(8,128)S(1)}, s32[4]{0:T(128)S(1)}, /*index=5*/s3...) while((s32[]{:T(128)}, f32[6,384]{1,0:T(8,128)S(1)}, ...), condition=%wide.region_5.6_spmd.clone, body=%wide.region_0.5_spmd.clone.sunk | while | flops 465526272 | bytes 17858036 | solution.py:80
  135.6 0.6 dynamic_slice.35
  138.1 0.7 dynamic_slice.36
  139.5 7.1 %conditional.3 = ((f32[6,384]{1,0:T(8,128)S(1)}, f32[6,384]{1,0:T(8,128)S(1)}, f32[6,384,128]{2,1,0:T(8,128)S(1)})) conditional(s32[]{:T(128)} %bitcast.55, (f32[6,384]{1,0:T(8,128)S(1)}, f32[6,384]{1,0:T(8,128)S(1)}, f32[6,384,128]{2,1,0:T(8,128)S(1)}) %tuple.48, (s32[384]{0:T(512)S(1)}, s32[]{:T(128)}, s32[]{:T(128)}, s32[4]{0:T(128)S(1)}, ...), branch_computations={%region_1.1_spmd, %region_2.4_spmd.clone} | conditional | flops 465525888 | bytes 17853058 | solution.py:70
  140.1 0.6 dynamic_slice.30
  140.9 0.8 abs_compare_fusion
  141.7 1.4 constant_dynamic-slice_fusion.1
  143.1 0.9 fusion.2
  144.0 0.9 fusion.4
  144.9 1.7 fusion.12
  146.6 0.6 dynamic_slice.35
  149.1 0.7 dynamic_slice.36
  150.4 7.1 %conditional.3 = ((f32[6,384]{1,0:T(8,128)S(1)}, f32[6,384]{1,0:T(8,128)S(1)}, f32[6,384,128]{2,1,0:T(8,128)S(1)})) conditional(s32[]{:T(128)} %bitcast.55, (f32[6,384]{1,0:T(8,128)S(1)}, f32[6,384]{1,0:T(8,128)S(1)}, f32[6,384,128]{2,1,0:T(8,128)S(1)}) %tuple.48, (s32[384]{0:T(512)S(1)}, s32[]{:T(128)}, s32[]{:T(128)}, s32[4]{0:T(128)S(1)}, ...), branch_computations={%region_1.1_spmd, %region_2.4_spmd.clone} | conditional | flops 465525888 | bytes 17853058 | solution.py:70
  151.1 0.6 dynamic_slice.30
  151.8 0.8 abs_compare_fusion
  152.7 1.4 constant_dynamic-slice_fusion.1
  154.0 0.9 fusion.2
  154.9 0.9 fusion.4
  155.8 1.7 fusion.12
  157.5 0.6 dynamic_slice.35
  160.1 0.7 dynamic_slice.36
  161.4 7.1 %conditional.3 = ((f32[6,384]{1,0:T(8,128)S(1)}, f32[6,384]{1,0:T(8,128)S(1)}, f32[6,384,128]{2,1,0:T(8,128)S(1)})) conditional(s32[]{:T(128)} %bitcast.55, (f32[6,384]{1,0:T(8,128)S(1)}, f32[6,384]{1,0:T(8,128)S(1)}, f32[6,384,128]{2,1,0:T(8,128)S(1)}) %tuple.48, (s32[384]{0:T(512)S(1)}, s32[]{:T(128)}, s32[]{:T(128)}, s32[4]{0:T(128)S(1)}, ...), branch_computations={%region_1.1_spmd, %region_2.4_spmd.clone} | conditional | flops 465525888 | bytes 17853058 | solution.py:70
  162.1 0.6 dynamic_slice.30
  162.8 0.8 abs_compare_fusion
  163.6 1.4 constant_dynamic-slice_fusion.1
  165.0 0.9 fusion.2
  165.9 0.9 fusion.4
  166.8 1.7 fusion.12
  168.5 0.6 dynamic_slice.35
  171.0 0.7 dynamic_slice.36
  172.4 7.1 %conditional.3 = ((f32[6,384]{1,0:T(8,128)S(1)}, f32[6,384]{1,0:T(8,128)S(1)}, f32[6,384,128]{2,1,0:T(8,128)S(1)})) conditional(s32[]{:T(128)} %bitcast.55, (f32[6,384]{1,0:T(8,128)S(1)}, f32[6,384]{1,0:T(8,128)S(1)}, f32[6,384,128]{2,1,0:T(8,128)S(1)}) %tuple.48, (s32[384]{0:T(512)S(1)}, s32[]{:T(128)}, s32[]{:T(128)}, s32[4]{0:T(128)S(1)}, ...), branch_computations={%region_1.1_spmd, %region_2.4_spmd.clone} | conditional | flops 465525888 | bytes 17853058 | solution.py:70
  173.0 0.6 dynamic_slice.30
  173.8 0.8 abs_compare_fusion
  174.6 1.4 constant_dynamic-slice_fusion.1
  176.0 0.9 fusion.2
  176.9 0.9 fusion.4
  177.8 1.7 fusion.12
  179.5 0.4 fusion.19
  179.9 0.4 copy.48
  180.3 0.7 convert_element_type.30
  181.0 11.2 %all_to_all.63 = bf16[1,8,48,768]{3,2,0,1:T(8,128)(2,1)S(1)} all-to-all(bf16[1,8,48,768]{3,2,0,1:T(8,128)(2,1)S(1)} %bitcast.70), channel_id=1, replica_groups=mesh['group'=2,'frame'=4,'space'=2,'head'=2] {'space'}, dimensions={1} | all-to-all | bytes 1179648 | tf_op jit(solution)/shard_map/all_to_all | solution.py:86
  192.2 0.9 copy.56
  (46 shorter events, 1.0 us)
Async XLA Ops:
  6.5 42.4 %copy-start = (s32[4,4]{1,0:T(4,128)S(1)}, s32[4,4]{1,0:T(4,128)}, u32[]{:S(2)}) copy-start(s32[4,4]{1,0:T(4,128)} %param.12) | copy-start | bytes 196
  6.5 9.5 %copy-start.1 = (bf16[1,4,48,1536]{3,2,1,0:T(8,128)(2,1)S(1)}, bf16[1,4,48,1536]{3,2,1,0:T(8,128)(2,1)}, u32[]{:S(2)}) copy-start(bf16[1,4,48,1536]{3,2,1,0:T(8,128)(2,1)} %param.10) | copy-start | bytes 1769476
  12.5 12.4 %all-to-all-start.1 = ((bf16[2,2,73728]{2,1,0:T(2,128)(2,1)}), bf16[2,2,73728]{2,1,0:T(2,128)(2,1)S(1)}, u32[]{:S(2)}, u32[]{:S(2)}) async-start(bf16[2,2,73728]{2,1,0:T(2,128)(2,1)} %reshape.68), calls=%async_computation.1 | async-start | bytes 1179648 | tf_op jit(solution)/shard_map/all_to_all | solution.py:49
  25.0 11.6 %all-to-all-start = ((bf16[2,2,73728]{2,1,0:T(2,128)(2,1)}), bf16[2,2,73728]{2,1,0:T(2,128)(2,1)S(1)}, u32[]{:S(2)}, u32[]{:S(2)}) async-start(bf16[2,2,73728]{2,1,0:T(2,128)(2,1)} %reshape.70), calls=%async_computation | async-start | bytes 1179648 | tf_op jit(solution)/shard_map/all_to_all | solution.py:48
  28.5 100.4 %all-gather.3.cloned.1.call-start = ((), (), s32[]{:S(2)}) async-start(), calls=%async_computation.4 | async-start | bytes 5898240 | tf_op jit(solution)/shard_map/all_gather | solution.py:64
  38.1 2.6 %copy-start.2 = (bf16[1,4,48,1536]{3,2,1,0:T(8,128)(2,1)S(1)}, bf16[1,4,48,1536]{3,2,1,0:T(8,128)(2,1)}, u32[]{:S(2)}) copy-start(bf16[1,4,48,1536]{3,2,1,0:T(8,128)(2,1)} %param.9) | copy-start | bytes 1769476
  45.2 10.7 %all-to-all-start.2 = ((bf16[2,2,73728]{2,1,0:T(2,128)(2,1)}), bf16[2,2,73728]{2,1,0:T(2,128)(2,1)S(1)}, u32[]{:S(2)}, u32[]{:S(2)}) async-start(bf16[2,2,73728]{2,1,0:T(2,128)(2,1)} %reshape.72), calls=%async_computation.2 | async-start | bytes 1179648 | tf_op jit(solution)/shard_map/all_to_all | solution.py:47
  128.8 6.7 %copy-start.3 = (s32[4]{0:T(128)S(1)}, s32[4]{0:T(128)}, u32[]{:S(2)}) copy-start(s32[4]{0:T(128)} %param.13) | copy-start | bytes 52
Sparse Core Ops, SparseCore 0:
  40.8 87.9 all-gather.2
where the time goes:
time: 201 us; the launch traced here: 200 us
  waiting for transfers between devices  86.3 us (43%)
  local copies, waits for them, and re-layouts  45.4 us (23%)
  between operations  13.6 us (7%)
  loops' own time  13.4 us (7%)
  blocking collectives  11.2 us (6%)
  starting transfers between devices  10.8 us (5%)
  matrix products  10.3 us (5%)
  other arithmetic  8.87 us (4%)
    all_gather x1, waiting for transfers between devices, shards(): key_piece = lax.all_gather(stacked, 'frame', axis=0, tiled=True)  69.8 us
    unnamed x19, local copies, waits for them, and re-layouts  26.3 us
    all_to_all x1, blocking collectives, shards(): lax.all_to_all(joined, 'space', split_axis=1, concat_axis=3, tiled=True)  11.2 us
    another operation x1, loops' own time, shards(): lax.scan(advance, initial, (key_piece, jnp.arange(key_piece.shape[0], dty...  10.5 us
    all_to_all x1, waiting for transfers between devices, shards(): lax.all_to_all(queries, 'space', split_axis=3, concat_axis=1, tiled=True)  6.99 us
    dot_general x4, matrix products, block_update(): jnp.einsum('hqk,khd->hqd', weights.astype(jnp.bfloat16), value_heads, pre...  6.73 us
    slice x4, local copies, waits for them, and re-layouts, block_update(): value_heads = key_block[1].reshape(key_count, head_count, head_size)  5.48 us
    all_to_all x1, waiting for transfers between devices, shards(): lax.all_to_all(keys, 'space', split_axis=3, concat_axis=1, tiled=True)  5.03 us
  transfers between devices with their start and end apart: 4, of which 4 were waited for; matrix products, arithmetic and copies ran while one was open for 7% of the time, Pallas kernels for 0%

commit v1 on v0

--- a/solution.py
+++ b/solution.py
@@ -61,7 +61,23 @@
     query_heads = head_query.reshape(frame_tokens, head_count, HEAD_DIM)
     flag_row = lax.dynamic_index_in_dim(flags, frame_now, 0, False)
     initial = empty_state((), head_count, frame_tokens)
-    key_piece = lax.all_gather(stacked, "frame", axis=0, tiled=True)
+    ways, here, hop = (lax.axis_size("frame"), lax.axis_index("frame"), stacked.shape[0])
+    shape = [n * ways if d == 0 else n for d, n in enumerate(stacked.shape)]
+    full = lax.dynamic_update_slice_in_dim(
+        jnp.zeros(shape, stacked.dtype), stacked, here * hop, axis=0
+    )
+    going_up = going_down = stacked
+    for far in range(1, ways // 2 + 1):
+        going_up = lax.ppermute(going_up, "frame", [(d, (d + 1) % ways) for d in range(ways)])
+        full = lax.dynamic_update_slice_in_dim(full, going_up, (here - far) % ways * hop, axis=0)
+        if 2 * far < ways:
+            going_down = lax.ppermute(
+                going_down, "frame", [(d, (d - 1) % ways) for d in range(ways)]
+            )
+            full = lax.dynamic_update_slice_in_dim(
+                full, going_down, (here + far) % ways * hop, axis=0
+            )
+    key_piece = full
 
     def advance(state_old, step_items):
         key_block, offset_now = step_items

time: 201 us -> 174 us (0.87)
  waiting for transfers between devices: 86.3 us -> 63.9 us
  between operations: 13.6 us -> 0.33 us
  local copies, waits for them, and re-layouts: 45.4 us -> 52.7 us
  starting transfers between devices: 10.8 us -> 14.4 us
    all_gather x1 -> x0, waiting for transfers between devices: 69.8 us -> none  [shards(): key_piece = lax.all_gather(stacked, 'frame', axis=0, tiled=True)]
    ppermute x0 -> x3, waiting for transfers between devices: none -> 49.5 us  [the longest x2 49.5 us: shards(): lax.ppermute(going_up, 'frame', [(d, (d + 1) % ways) for d in range(ways)])]
    unnamed x19 -> x18, local copies, waits for them, and re-layouts: 26.3 us -> 19.6 us
    ppermute x0 -> x3, local copies, waits for them, and re-layouts: none -> 5.1 us  [the longest x2 3.4 us: shards(): lax.ppermute(going_up, 'frame', [(d, (d + 1) % ways) for d in range(ways)])]
    dynamic_update_slice x0 -> x4, local copies, waits for them, and re-layouts: none -> 4.61 us  [the longest x2 2.31 us: shards(): lax.dynamic_update_slice_in_dim(full, going_up, (here - far) % ways * hop...]
    broadcast_in_dim x0 -> x2, local copies, waits for them, and re-layouts: none -> 4.23 us  [the longest x1 2.53 us: shards(): jnp.zeros(shape, stacked.dtype)]
    ppermute x0 -> x3, starting transfers between devices: none -> 3.71 us  [the longest x2 3.26 us: shards(): lax.ppermute(going_up, 'frame', [(d, (d + 1) % ways) for d in range(ways)])]
    all_to_all x1, waiting for transfers between devices: 6.99 us -> 4.94 us  [shards(): lax.all_to_all(queries, 'space', split_axis=3, concat_axis=1, tiled=True)]
  transfers between devices with their start and end apart: 4 -> 6, of which waited for: 4 -> 4; matrix products, arithmetic and copies ran while one was open for 7% -> 15% of each run, Pallas kernels for 0% -> 0%
where the time goes in v1:
time: 174 us; the launch traced here: 173 us
  waiting for transfers between devices  63.9 us (37%)
  local copies, waits for them, and re-layouts  52.7 us (30%)
  starting transfers between devices  14.4 us (8%)
  loops' own time  13.4 us (8%)
  matrix products  10.2 us (6%)
  blocking collectives  9.35 us (5%)
  other arithmetic  8.92 us (5%)
    ppermute x2, waiting for transfers between devices, shards(): lax.ppermute(going_up, 'frame', [(d, (d + 1) % ways) for d in range(ways)])  49.5 us
    unnamed x18, local copies, waits for them, and re-layouts  19.6 us
    another operation x1, loops' own time, shards(): lax.scan(advance, initial, (key_piece, jnp.arange(key_piece.shape[0], dty...  10.5 us
    all_to_all x1, blocking collectives, shards(): lax.all_to_all(joined, 'space', split_axis=1, concat_axis=3, tiled=True)  9.35 us
    dot_general x4, matrix products, block_update(): jnp.einsum('hqk,khd->hqd', weights.astype(jnp.bfloat16), value_heads, pre...  6.68 us
    slice x4, local copies, waits for them, and re-layouts, block_update(): value_heads = key_block[1].reshape(key_count, head_count, head_size)  5.48 us
    all_to_all x1, waiting for transfers between devices, shards(): lax.all_to_all(keys, 'space', split_axis=3, concat_axis=1, tiled=True)  5.07 us
    all_to_all x1, waiting for transfers between devices, shards(): lax.all_to_all(queries, 'space', split_axis=3, concat_axis=1, tiled=True)  4.94 us
  transfers between devices with their start and end apart: 6, of which 4 were waited for; matrix products, arithmetic and copies ran while one was open for 15% of the time, Pallas kernels for 0%

profile of v1, /device:TPU:16, one launch (start us, length us, event | category | flops | bytes accessed | tf_op | source)
XLA Modules:
  0.0 173.3 jit_solution(11444955918683720375)
XLA Ops:
  0.0 2.6 %copy.47 = bf16[1,4,48,1536]{2,1,0,3:T(4,128)(2,1)S(1)} copy(bf16[1,4,48,1536]{3,2,1,0:T(8,128)(2,1)} %param.11) | data formatting | bytes 1179648 | tf_op args[2]
  2.6 3.4 %reshape.67 = bf16[2,2,73728]{2,1,0:T(2,128)(2,1)} reshape(bf16[1536,1,4,48]{3,2,1,0:T(4,128)(2,1)S(1)} %bitcast.62) | data formatting | bytes 1179648
  6.0 3.5 %all-to-all-start.1 = ((bf16[2,2,73728]{2,1,0:T(2,128)(2,1)}), bf16[2,2,73728]{2,1,0:T(2,128)(2,1)S(1)}, u32[]{:S(2)}, u32[]{:S(2)}) async-start(bf16[2,2,73728]{2,1,0:T(2,128)(2,1)} %reshape.67), calls=%async_computation.1 | async-start | bytes 1179648 | tf_op jit(solution)/shard_map/all_to_all | solution.py:49
  9.5 1.1 copy.44
  10.6 3.4 %reshape.69 = bf16[2,2,73728]{2,1,0:T(2,128)(2,1)} reshape(bf16[1536,1,4,48]{3,2,1,0:T(4,128)(2,1)S(1)} %bitcast.63) | data formatting | bytes 1179648
  14.0 4.5 %all-to-all-done.1 = bf16[2,2,73728]{2,1,0:T(2,128)(2,1)S(1)} async-done(((bf16[2,2,73728]{2,1,0:T(2,128)(2,1)}), bf16[2,2,73728]{2,1,0:T(2,128)(2,1)S(1)}, u32[]{:S(2)}, u32[]{:S(2)}) %all-to-all-start.1) | async-done | bytes 589856 | tf_op jit(solution)/shard_map/all_to_all | solution.py:49
  18.4 3.5 %all-to-all-start = ((bf16[2,2,73728]{2,1,0:T(2,128)(2,1)}), bf16[2,2,73728]{2,1,0:T(2,128)(2,1)S(1)}, u32[]{:S(2)}, u32[]{:S(2)}) async-start(bf16[2,2,73728]{2,1,0:T(2,128)(2,1)} %reshape.69), calls=%async_computation | async-start | bytes 1179648 | tf_op jit(solution)/shard_map/all_to_all | solution.py:48
  21.9 1.6 reshape.68
  23.5 1.3 copy.64
  24.9 5.1 %all-to-all-done = bf16[2,2,73728]{2,1,0:T(2,128)(2,1)S(1)} async-done(((bf16[2,2,73728]{2,1,0:T(2,128)(2,1)}), bf16[2,2,73728]{2,1,0:T(2,128)(2,1)S(1)}, u32[]{:S(2)}, u32[]{:S(2)}) %all-to-all-start) | async-done | bytes 589856 | tf_op jit(solution)/shard_map/all_to_all | solution.py:48
  30.0 1.6 reshape.70
  31.6 1.3 copy.63
  33.0 1.2 maximum_bitcast_fusion
  34.2 1.6 collective-permute-start
  36.2 49.5 %collective-permute-done = bf16[1,2,384,768]{3,2,1,0:T(8,128)(2,1)} collective-permute-done((bf16[1,2,384,768]{3,2,1,0:T(8,128)(2,1)}, bf16[1,2,384,768]{3,2,1,0:T(8,128)(2,1)}, u32[]{:S(2)}, u32[]{:S(2)}) %collective-permute-start) | collective-permute-done | bytes 1179680 | tf_op jit(solution)/shard_map/ppermute | solution.py:71
  85.6 1.7 collective-permute-start.2
  87.3 1.0 copy.54
  88.4 3.4 %reshape.71 = bf16[2,2,73728]{2,1,0:T(2,128)(2,1)} reshape(bf16[1536,1,4,48]{3,2,1,0:T(4,128)(2,1)S(1)} %bitcast.64) | data formatting | bytes 1179648
  91.8 3.7 %all-to-all-start.2 = ((bf16[2,2,73728]{2,1,0:T(2,128)(2,1)}), bf16[2,2,73728]{2,1,0:T(2,128)(2,1)S(1)}, u32[]{:S(2)}, u32[]{:S(2)}) async-start(bf16[2,2,73728]{2,1,0:T(2,128)(2,1)} %reshape.71), calls=%async_computation.2 | async-start | bytes 1179648 | tf_op jit(solution)/shard_map/all_to_all | solution.py:47
  95.6 1.7 copy.50
  97.3 4.9 %all-to-all-done.2 = bf16[2,2,73728]{2,1,0:T(2,128)(2,1)S(1)} async-done(((bf16[2,2,73728]{2,1,0:T(2,128)(2,1)}), bf16[2,2,73728]{2,1,0:T(2,128)(2,1)S(1)}, u32[]{:S(2)}, u32[]{:S(2)}) %all-to-all-start.2) | async-done | bytes 589856 | tf_op jit(solution)/shard_map/all_to_all | solution.py:47
  102.2 1.6 reshape.72
  103.8 0.8 copy.55
  104.5 0.7 reshape.64
  105.3 2.5 %broadcast_in_dim.50 = bf16[4,2,384,768]{2,3,1,0:T(8,128)(2,1)} broadcast(bf16[]{:T(256)} %constant.83.clone.1), dimensions={} | broadcast | bytes 4718594 | tf_op jit(solution)/shard_map/broadcast_in_dim | solution.py:67
  107.8 1.2 constant_dynamic-update-slice_fusion.3
  109.0 1.7 copy.51
  110.7 1.7 copy.52
  112.4 1.1 constant_dynamic-update-slice_fusion.2
  113.6 1.2 constant_dynamic-update-slice_fusion.1
  114.7 1.7 copy.53
  116.4 1.2 constant_dynamic-update-slice_fusion
  117.7 43.9 %while.15 = (s32[]{:T(128)}, f32[6,384]{1,0:T(8,128)S(1)}, f32[6,384]{1,0:T(8,128)S(1)}, f32[6,384,128]{2,1,0:T(8,128)S(1)}, s32[4]{0:T(128)S(1)}, /*index=5*/s3...) while((s32[]{:T(128)}, f32[6,384]{1,0:T(8,128)S(1)}, ...), condition=%wide.region_5.6_spmd.clone, body=%wide.region_0.5_spmd.clone.sunk | while | flops 465526272 | bytes 17858036 | solution.py:96
  120.2 0.7 dynamic_slice.38
  121.6 7.1 %conditional.3 = ((f32[6,384]{1,0:T(8,128)S(1)}, f32[6,384]{1,0:T(8,128)S(1)}, f32[6,384,128]{2,1,0:T(8,128)S(1)})) conditional(s32[]{:T(128)} %bitcast.56, (f32[6,384]{1,0:T(8,128)S(1)}, f32[6,384]{1,0:T(8,128)S(1)}, f32[6,384,128]{2,1,0:T(8,128)S(1)}) %tuple.48, (s32[384]{0:T(512)S(1)}, s32[]{:T(128)}, s32[]{:T(128)}, s32[4]{0:T(128)S(1)}, ...), branch_computations={%region_1.1_spmd, %region_2.4_spmd.clone} | conditional | flops 465525888 | bytes 17853058 | solution.py:86
  123.0 0.8 abs_compare_fusion
  123.8 1.4 constant_dynamic-slice_fusion.1
  125.2 0.9 fusion.2
  126.1 0.9 fusion.4
  127.0 1.7 fusion.12
  131.2 0.7 dynamic_slice.38
  132.5 7.1 %conditional.3 = ((f32[6,384]{1,0:T(8,128)S(1)}, f32[6,384]{1,0:T(8,128)S(1)}, f32[6,384,128]{2,1,0:T(8,128)S(1)})) conditional(s32[]{:T(128)} %bitcast.56, (f32[6,384]{1,0:T(8,128)S(1)}, f32[6,384]{1,0:T(8,128)S(1)}, f32[6,384,128]{2,1,0:T(8,128)S(1)}) %tuple.48, (s32[384]{0:T(512)S(1)}, s32[]{:T(128)}, s32[]{:T(128)}, s32[4]{0:T(128)S(1)}, ...), branch_computations={%region_1.1_spmd, %region_2.4_spmd.clone} | conditional | flops 465525888 | bytes 17853058 | solution.py:86
  133.9 0.8 abs_compare_fusion
  134.8 1.4 constant_dynamic-slice_fusion.1
  136.1 0.9 fusion.2
  137.0 0.9 fusion.4
  137.9 1.7 fusion.12
  142.2 0.7 dynamic_slice.38
  143.5 7.1 %conditional.3 = ((f32[6,384]{1,0:T(8,128)S(1)}, f32[6,384]{1,0:T(8,128)S(1)}, f32[6,384,128]{2,1,0:T(8,128)S(1)})) conditional(s32[]{:T(128)} %bitcast.56, (f32[6,384]{1,0:T(8,128)S(1)}, f32[6,384]{1,0:T(8,128)S(1)}, f32[6,384,128]{2,1,0:T(8,128)S(1)}) %tuple.48, (s32[384]{0:T(512)S(1)}, s32[]{:T(128)}, s32[]{:T(128)}, s32[4]{0:T(128)S(1)}, ...), branch_computations={%region_1.1_spmd, %region_2.4_spmd.clone} | conditional | flops 465525888 | bytes 17853058 | solution.py:86
  144.9 0.8 abs_compare_fusion
  145.7 1.4 constant_dynamic-slice_fusion.1
  147.1 0.9 fusion.2
  148.0 0.9 fusion.4
  148.9 1.7 fusion.12
  153.1 0.7 dynamic_slice.38
  154.5 7.1 %conditional.3 = ((f32[6,384]{1,0:T(8,128)S(1)}, f32[6,384]{1,0:T(8,128)S(1)}, f32[6,384,128]{2,1,0:T(8,128)S(1)})) conditional(s32[]{:T(128)} %bitcast.56, (f32[6,384]{1,0:T(8,128)S(1)}, f32[6,384]{1,0:T(8,128)S(1)}, f32[6,384,128]{2,1,0:T(8,128)S(1)}) %tuple.48, (s32[384]{0:T(512)S(1)}, s32[]{:T(128)}, s32[]{:T(128)}, s32[4]{0:T(128)S(1)}, ...), branch_computations={%region_1.1_spmd, %region_2.4_spmd.clone} | conditional | flops 465525888 | bytes 17853058 | solution.py:86
  155.8 0.8 abs_compare_fusion
  156.7 1.4 constant_dynamic-slice_fusion.1
  158.1 0.9 fusion.2
  159.0 0.9 fusion.4
  159.9 1.7 fusion.12
  162.4 0.7 convert_element_type.30
  163.0 9.3 %all_to_all.63 = bf16[1,8,48,768]{3,2,0,1:T(8,128)(2,1)S(1)} all-to-all(bf16[1,8,48,768]{3,2,0,1:T(8,128)(2,1)S(1)} %bitcast.70), channel_id=1, replica_groups=mesh['group'=2,'frame'=4,'space'=2,'head'=2] {'space'}, dimensions={1} | all-to-all | bytes 1179648 | tf_op jit(solution)/shard_map/all_to_all | solution.py:102
  172.4 0.9 copy.65
  (57 shorter events, 6.9 us)
Async XLA Ops:
  0.0 95.5 %copy-start = (s32[4,4]{1,0:T(4,128)S(1)}, s32[4,4]{1,0:T(4,128)}, u32[]{:S(2)}) copy-start(s32[4,4]{1,0:T(4,128)} %param.12) | copy-start | bytes 196
  0.0 9.5 %copy-start.1 = (bf16[1,4,48,1536]{3,2,1,0:T(8,128)(2,1)S(1)}, bf16[1,4,48,1536]{3,2,1,0:T(8,128)(2,1)}, u32[]{:S(2)}) copy-start(bf16[1,4,48,1536]{3,2,1,0:T(8,128)(2,1)} %param.10) | copy-start | bytes 1769476
  6.0 12.4 %all-to-all-start.1 = ((bf16[2,2,73728]{2,1,0:T(2,128)(2,1)}), bf16[2,2,73728]{2,1,0:T(2,128)(2,1)S(1)}, u32[]{:S(2)}, u32[]{:S(2)}) async-start(bf16[2,2,73728]{2,1,0:T(2,128)(2,1)} %reshape.67), calls=%async_computation.1 | async-start | bytes 1179648 | tf_op jit(solution)/shard_map/all_to_all | solution.py:49
  18.4 11.6 %all-to-all-start = ((bf16[2,2,73728]{2,1,0:T(2,128)(2,1)}), bf16[2,2,73728]{2,1,0:T(2,128)(2,1)S(1)}, u32[]{:S(2)}, u32[]{:S(2)}) async-start(bf16[2,2,73728]{2,1,0:T(2,128)(2,1)} %reshape.69), calls=%async_computation | async-start | bytes 1179648 | tf_op jit(solution)/shard_map/all_to_all | solution.py:48
  24.9 62.4 %copy-start.2 = (bf16[1,4,48,1536]{3,2,1,0:T(8,128)(2,1)S(1)}, bf16[1,4,48,1536]{3,2,1,0:T(8,128)(2,1)}, u32[]{:S(2)}) copy-start(bf16[1,4,48,1536]{3,2,1,0:T(8,128)(2,1)} %param.9) | copy-start | bytes 1769476
  34.2 51.5 %collective-permute-start = (bf16[1,2,384,768]{3,2,1,0:T(8,128)(2,1)}, bf16[1,2,384,768]{3,2,1,0:T(8,128)(2,1)}, u32[]{:S(2)}, u32[]{:S(2)}) collective-permute-start(bf16[1,2,384,768]{3,2,1,0:T(8,128)(2,1)} %maximum_bitcast_fusion), channel_id=1, source_target_pairs={{0,4},{4,8},{8,12},{12,0},{1,5},{5,9},{9,13},{13,1},{2,6},{6,10},{... | collective-permute-start | bytes 3538952 | tf_op jit(solution)/shard_map/ppermute | solution.py:71
  35.7 75.0 %collective-permute-start.1 = (bf16[1,2,384,768]{3,2,1,0:T(8,128)(2,1)}, bf16[1,2,384,768]{3,2,1,0:T(8,128)(2,1)}, u32[]{:S(2)}, u32[]{:S(2)}) collective-permute-start(bf16[1,2,384,768]{3,2,1,0:T(8,128)(2,1)} %maximum_bitcast_fusion), channel_id=1, source_target_pairs={{0,12},{4,0},{8,4},{12,8},{1,13},{5,1},{9,5},{13,9},{2,14},{6,2},{... | collective-permute-start | bytes 3538952 | tf_op jit(solution)/shard_map/ppermute | solution.py:74
  85.6 29.1 %collective-permute-start.2 = (bf16[1,2,384,768]{3,2,1,0:T(8,128)(2,1)}, bf16[1,2,384,768]{3,2,1,0:T(8,128)(2,1)}, u32[]{:S(2)}, u32[]{:S(2)}) collective-permute-start(bf16[1,2,384,768]{3,2,1,0:T(8,128)(2,1)} %collective-permute-done), channel_id=1, source_target_pairs={{0,4},{4,8},{8,12},{12,0},{1,5},{5,9},{9,13},{13,1},{2,6},{6,10},{... | collective-permute-start | bytes 3538952 | tf_op jit(solution)/shard_map/ppermute | solution.py:71
  91.8 10.4 %all-to-all-start.2 = ((bf16[2,2,73728]{2,1,0:T(2,128)(2,1)}), bf16[2,2,73728]{2,1,0:T(2,128)(2,1)S(1)}, u32[]{:S(2)}, u32[]{:S(2)}) async-start(bf16[2,2,73728]{2,1,0:T(2,128)(2,1)} %reshape.71), calls=%async_computation.2 | async-start | bytes 1179648 | tf_op jit(solution)/shard_map/all_to_all | solution.py:47
  114.7 3.0 %copy-start.3 = (s32[4]{0:T(128)S(1)}, s32[4]{0:T(128)}, u32[]{:S(2)}) copy-start(s32[4]{0:T(128)} %param.13) | copy-start | bytes 52
